TPU v7x, 128 devices: a whole 4x4x4 slice. The times are simulated.
128 devices in a mesh: ctx: 32 (over z, x, core), exp: 4 (over y).
Axes of the slice: x: 4, y: 4, z: 4, core: 2. Of those that a mesh axis runs over, the one named last changes fastest.
Arguments:
- queries: bfloat16 [8192, 4096], P('ctx', 'exp'), may hold values from -6 to 6
- key_rows: bfloat16 [8192, 4096], P('ctx', 'exp'), may hold values from -6 to 6
- value_rows: bfloat16 [8192, 4096], P('ctx', 'exp'), may hold values from -6 to 6
- gate_rows: bfloat16 [8192, 4096], P('ctx', 'exp'), may hold values from -6 to 6
- decay_exp: int32 [32], P('exp'), may hold values from 5 to 16
- attn_gain: float32 [4096], P('exp'), may hold values from 0.1 to 1.9
- out_proj: bfloat16 [4096, 6144], P('exp'), may hold values from -0.09375 to 0.09375
- residual: bfloat16 [8192, 6144], P(('ctx', 'exp')), may hold values from -6 to 6
- norm_gain: float32 [6144], replicated, may hold values from 0.1 to 1.9
- routes: int32 [8192, 2], P('ctx'), may hold values from 0 to 31, as said below
- route_weights: float32 [8192, 2], P('ctx'), may hold values from 0.1 to 1
- w_gate: bfloat16 [4, 9216, 6144], P('exp', 'ctx'), may hold values from -0.078125 to 0.078125
- w_up: bfloat16 [4, 9216, 6144], P('exp', 'ctx'), may hold values from -0.078125 to 0.078125
- w_down: bfloat16 [4, 9216, 6144], P('exp', 'ctx'), may hold values from -0.0625 to 0.0625
Outputs:
- layer_out: bfloat16 [8192, 6144], P(('ctx', 'exp'))
Inputs may be any that keep to these rules, and one draw needn't show every extreme that they name: `routes`: A row's two entries differ. An expert e below 4 is named only in column e % 2. In every aligned block of 64 rows each expert below 4 is named at most 8 times, and some expert below 4 exactly 8 times.
All inputs are finite; a program needn't handle non-finite values.
Results may differ from a plain program's by a relative error of at most 0.018.
Values may be sent and summed in bfloat16 or wider, within the bound.
A program may use at most 128 MiB of HBM per device.

v0:
```python
import jax
import jax.numpy as jnp
from jax import lax
from jax.sharding import PartitionSpec as P

EPSILON = 1e-06


def earlier_states(update, decay_rates, row_count):
    size, index = (lax.axis_size("ctx"), lax.axis_index("ctx"))
    everything = lax.all_gather(update.astype(jnp.bfloat16), "ctx").astype(jnp.float32)
    distance = (index - 1 - jnp.arange(size)).astype(jnp.float32)
    factors = jnp.where(
        distance[:, None] >= 0.0,
        jnp.exp(-decay_rates[None, :] * row_count * jnp.maximum(distance, 0.0)[:, None]),
        0.0,
    )
    return jnp.sum(everything * factors[:, :, None, None], axis=0)


def span_local(queries, key_rows, value_rows, decay_exp):
    row_count = queries.shape[0]
    head_count = decay_exp.shape[0]
    head_width = queries.shape[1] // head_count
    query_heads = queries.reshape(row_count, head_count, head_width)
    key_heads = key_rows.reshape(row_count, head_count, head_width)
    value_heads = value_rows.reshape(row_count, head_count, head_width)
    decay_rates = jnp.exp2(-decay_exp.astype(jnp.float32))
    positions = jnp.arange(row_count, dtype=jnp.float32)
    offsets = positions[:, None] - positions[None, :]
    damping = jnp.where(
        offsets[None] >= 0.0,
        jnp.exp(-decay_rates[:, None, None] * jnp.maximum(offsets, 0.0)[None]),
        0.0,
    )
    scores = jnp.einsum("thd,shd->hts", query_heads, key_heads, preferred_element_type=jnp.float32)
    mixing = (scores * damping).astype(jnp.bfloat16)
    inner_part = jnp.einsum("hts,shd->thd", mixing, value_heads, preferred_element_type=jnp.float32)
    tail_decay = jnp.exp(-decay_rates[None, :] * (row_count - 1.0 - positions)[:, None])
    keyed_rows = (key_heads.astype(jnp.float32) * tail_decay[:, :, None]).astype(jnp.bfloat16)
    update = jnp.einsum("shd,she->hde", keyed_rows, value_heads, preferred_element_type=jnp.float32)
    lead_decay = jnp.exp(-decay_rates[None, :] * (positions + 1.0)[:, None])
    leading = query_heads.astype(jnp.float32) * lead_decay[:, :, None]
    return (inner_part, leading, update, decay_rates)


def settle(inner_part, leading, prior_state, gate_rows, attn_gain):
    outer_part = jnp.einsum("thd,hde->the", leading, prior_state, precision=lax.Precision.HIGHEST)
    mixed_heads = inner_part + outer_part
    row_count, head_count, head_width = mixed_heads.shape
    mean_square = jnp.mean(mixed_heads * mixed_heads, axis=2, keepdims=True)
    normed_heads = mixed_heads * lax.rsqrt(mean_square + EPSILON)
    gain_heads = attn_gain.reshape(head_count, head_width)
    gate_heads = gate_rows.reshape(row_count, head_count, head_width).astype(jnp.float32)
    settled = (normed_heads * gain_heads * jax.nn.sigmoid(gate_heads)).astype(jnp.bfloat16)
    return settled.reshape(row_count, head_count * head_width)


def token_norm(hidden, norm_gain):
    mean_square = jnp.mean(hidden * hidden, axis=1, keepdims=True)
    return (hidden * lax.rsqrt(mean_square + EPSILON) * norm_gain).astype(jnp.bfloat16)


def slot_table(chosen_ids, expert_count, capacity):
    owners = jnp.arange(expert_count, dtype=jnp.int32)
    chosen = jnp.where(owners[:, None] % 2 == 0, chosen_ids[None, :, 0], chosen_ids[None, :, 1])
    picked = chosen == owners[:, None]
    row_count = chosen_ids.shape[0]
    upto = jnp.arange(row_count)[:, None] <= jnp.arange(row_count)[None, :]
    slot_rank = jnp.dot(picked.astype(jnp.float32), upto.astype(jnp.float32)) - 1.0
    slot_ids = jnp.arange(capacity, dtype=jnp.float32)
    return picked[:, None, :] & (slot_rank[:, None, :] == slot_ids[None, :, None])


def expert_part(slot_rows, gate_cols, up_cols, down_rows):
    contract_dims = (((1,), (1,)), ((), ()))
    first_half = lax.dot_general(
        slot_rows, gate_cols, contract_dims, preferred_element_type=jnp.float32
    )
    second_half = lax.dot_general(
        slot_rows, up_cols, contract_dims, preferred_element_type=jnp.float32
    )
    activated = (jax.nn.silu(first_half) * second_half).astype(jnp.bfloat16)
    return jnp.dot(activated, down_rows, preferred_element_type=jnp.float32)


def body(
    queries,
    key_rows,
    value_rows,
    gate_rows,
    decay_exp,
    attn_gain,
    out_proj,
    residual,
    norm_gain,
    routes,
    route_weights,
    w_gate,
    w_up,
    w_down,
):
    inner_part, leading, update, decay_rates = span_local(queries, key_rows, value_rows, decay_exp)
    span_rows = queries.shape[0]
    prior_state = earlier_states(update, decay_rates, span_rows)
    settled = settle(inner_part, leading, prior_state, gate_rows, attn_gain)
    group_count = lax.axis_size("exp")
    group_rows = span_rows // group_count
    first_mine = lax.axis_index("exp") * group_rows
    capacity = group_rows // 8
    projected = jnp.dot(settled, out_proj, preferred_element_type=jnp.float32)
    summed = lax.psum_scatter(
        projected.astype(jnp.bfloat16), "exp", scatter_dimension=0, tiled=True
    ).astype(jnp.float32)
    hidden = summed + residual.astype(jnp.float32)
    normed = token_norm(hidden, norm_gain)
    my_routes = lax.dynamic_slice_in_dim(routes, first_mine, group_rows, 0)
    my_weights = lax.dynamic_slice_in_dim(route_weights, first_mine, group_rows, 0)
    table = slot_table(my_routes, group_count, capacity)
    outgoing = jnp.einsum(
        "ecn,nd->ecd", table.astype(jnp.bfloat16), normed, preferred_element_type=jnp.float32
    ).astype(jnp.bfloat16)
    mine = lax.all_to_all(outgoing, "exp", 0, 0, tiled=True)
    mine = mine.reshape(group_count * capacity, -1)
    gathered = lax.all_gather(mine, "ctx", axis=0, tiled=True)
    produced = lax.psum_scatter(
        expert_part(gathered, w_gate[0], w_up[0], w_down[0]).astype(jnp.bfloat16),
        "ctx",
        scatter_dimension=0,
        tiled=True,
    )
    produced = produced.reshape(group_count, capacity, -1)
    returned = lax.all_to_all(produced, "exp", 0, 0, tiled=True)
    for column in range(2):
        fetched = jnp.einsum(
            "ecn,ecd->nd",
            table[column::2].astype(jnp.bfloat16),
            returned[column::2],
            preferred_element_type=jnp.float32,
        )
        hidden = hidden + my_weights[:, column][:, None] * fetched
    return hidden.astype(jnp.bfloat16)


def solution(mesh):
    in_specs = (
        P("ctx", "exp"),
        P("ctx", "exp"),
        P("ctx", "exp"),
        P("ctx", "exp"),
        P("exp"),
        P("exp"),
        P("exp", None),
        P(("ctx", "exp"), None),
        P(),
        P("ctx", None),
        P("ctx", None),
        P("exp", "ctx", None),
        P("exp", "ctx", None),
        P("exp", "ctx", None),
    )
    out_specs = P(("ctx", "exp"), None)
    return jax.shard_map(body, mesh=mesh, in_specs=in_specs, out_specs=out_specs, check_vma=False)
```

profile of v0, /device:TPU:0, one launch (start us, length us, event | category | flops | bytes accessed | tf_op | source)
XLA Modules:
  0.0 362.1 jit_solution(7711785279852202598)
XLA Ops:
  6.5 0.0 copy-start
  6.5 0.0 all-gather.6.cloned.1.call-start
  6.5 1.4 broadcast_multiply_fusion
  7.9 2.0 copy.27
  10.0 0.7 multiply_exponential_fusion
  10.7 2.2 convolution_convert_fusion.3
  12.9 0.0 all-gather.6.cloned.1.call-update
  12.9 0.0 reduce-scatter.3.cloned.1.call-start
  13.0 2.3 add_divide_fusion
  15.2 0.0 copy-done.6
  15.2 2.6 copy.25
  17.9 0.7 fusion.46
  18.6 0.8 fusion.45
  19.4 0.7 exponential_select_fusion
  20.1 48.4 %all-gather.6.cloned.1.call-done = bf16[256,128,128]{2,1,0:T(8,128)(2,1)} async-done(((bf16[8,128,128]{2,1,0:T(8,128)(2,1)}), bf16[256,128,128]{2,1,0:T(8,128)(2,1)}) %all-gather.6.cloned.1.call-update) | async-done | bytes 8388624 | tf_op jit(solution)/shard_map/all_gather | solution.py:11
  68.5 5.2 %fusion = f32[8,128,128]{2,1,0:T(8,128)S(1)} fusion(bf16[32,8,128,128]{3,2,1,0:T(8,128)(2,1)} %bitcast.93, f32[32,8]{1,0:T(8,128)S(1)} %exponential_select_fusion), kind=kLoop, calls=%fused_computation.1 | loop fusion | flops 12451840 | bytes 8913920 | tf_op jit(solution)/shard_map/reduce_sum | solution.py:18
  73.7 0.0 copy-start.7
  73.7 0.0 copy-done.3
  73.7 0.0 copy-done.4
  73.7 2.4 convolution_bitcast_fusion.2
  76.1 3.7 %multiply_reduce_fusion.1 = (f32[256,8]{0,1:T(8,128)S(1)}, f32[256,8,128]{0,2,1:T(8,128)}) fusion(f32[256,8,128]{0,2,1:T(8,128)} %convolution_bitcast_fusion.2, bf16[256,8,128]{0,2,1:T(8,128)(2,1)} %bitcast.98, f32[256,256]{1,0:T(8,128)} %fusion.45, f32[8]{0:T(128)S(1)} %copy-done.7, pred[256,256]{1,0:T(8,128)(4,1)} %fusion.46, ...), kind=kOutput, calls=%fused_computation.31 | convolution fusion | flops 271316992 | bytes 4005920 | tf_op jit(solution)/shard_map/hts,shd->thd/dot_general | solution.py:38
  79.8 1.8 multiply_convert_fusion.2
  81.6 9.5 %convolution_convert_fusion.1 = bf16[256,6144]{1,0:T(8,128)(2,1)} fusion(bf16[256,1024]{0,1:T(8,128)(2,1)S(1)} %bitcast.95, bf16[1024,6144]{1,0:T(8,128)(2,1)} %param.20), kind=kOutput, calls=%fused_computation.3 | convolution fusion | flops 3222798336 | bytes 16252928 | tf_op jit(solution)/shard_map/dot_general | solution.py:111
  91.1 0.0 reduce-scatter.3.cloned.1.call-update
  91.1 0.0 all-gather.4.cloned.1.call-start
  91.2 0.6 copy-done.8
  91.8 0.1 constant_dynamic-slice_fusion
  91.9 0.1 iota_compare_fusion.3
  91.9 0.1 convolution_add_fusion
  92.1 37.0 %reduce-scatter.3.cloned.1.call-done = bf16[64,6144]{1,0:T(8,128)(2,1)} async-done(((bf16[256,6144]{1,0:T(8,128)(2,1)}), bf16[64,6144]{1,0:T(8,128)(2,1)}) %reduce-scatter.3.cloned.1.call-update) | async-done | bytes 786448 | tf_op jit(solution)/shard_map/reduce_scatter | solution.py:112
  129.1 1.7 multiply_reduce_fusion
  130.9 1.8 convolution_convert_fusion.2
  132.7 11.5 %all_to_all.10 = bf16[4,8,6144]{2,1,0:T(8,128)(2,1)} all-to-all(bf16[4,8,6144]{2,1,0:T(8,128)(2,1)S(1)} %convolution_convert_fusion.2), channel_id=1, replica_groups=mesh['ctx'=32,'exp'=4] {'exp'}, dimensions={0} | all-to-all | bytes 786432 | tf_op jit(solution)/shard_map/all_to_all | solution.py:123
  144.2 0.0 all-gather.4.cloned.1.call-update
  144.2 0.2 reduce-scatter.5.cloned.1.call-start
  144.4 62.3 %all-gather.4.cloned.1.call-done = bf16[1024,6144]{1,0:T(8,128)(2,1)} async-done(((bf16[32,6144]{1,0:T(8,128)(2,1)}), bf16[1024,6144]{1,0:T(8,128)(2,1)}) %all-gather.4.cloned.1.call-update) | async-done | bytes 12582928 | tf_op jit(solution)/shard_map/all_gather | solution.py:125
  206.7 10.5 %fusion.9 = f32[1024,288]{0,1:T(8,128)} fusion(bf16[1024,6144]{1,0:T(8,128)(2,1)} %all-gather.4.cloned.1.call-done, bf16[1,288,6144]{2,1,0:T(8,128)(2,1)} %param.25), kind=kOutput, calls=%fused_computation.15 | convolution fusion | flops 3623878656 | bytes 17301504 | tf_op jit(solution)/shard_map/dot_general | solution.py:77
  217.2 17.6 %convolution_convert_fusion = bf16[1024,6144]{1,0:T(8,128)(2,1)} fusion(bf16[1,288,6144]{2,1,0:T(8,128)(2,1)S(1)} %copy-done, bf16[1024,6144]{1,0:T(8,128)(2,1)} %all-gather.4.cloned.1.call-done, bf16[1,288,6144]{2,1,0:T(8,128)(2,1)} %param.26, f32[1024,288]{0,1:T(8,128)} %fusion.9), kind=kOutput, calls=%fused_computation.2 | convolution fusion | flops 7255818240 | bytes 33423360 | tf_op jit(solution)/shard_map/dot_general | solution.py:84
  234.8 0.0 reduce-scatter.5.cloned.1.call-update
  234.9 0.7 copy-done.9
  235.5 0.1 constant_dynamic-slice_fusion.1
  235.6 103.3 %reduce-scatter.5.cloned.1.call-done = bf16[32,6144]{1,0:T(8,128)(2,1)} async-done(((bf16[1024,6144]{1,0:T(8,128)(2,1)}), bf16[32,6144]{1,0:T(8,128)(2,1)}) %reduce-scatter.5.cloned.1.call-update) | async-done | bytes 393232 | tf_op jit(solution)/shard_map/reduce_scatter | solution.py:126
  338.9 4.3 %all-to-all-start.1 = ((bf16[4,8,6144]{2,1,0:T(8,128)(2,1)}), bf16[4,8,6144]{2,1,0:T(8,128)(2,1)S(1)}, u32[]{:S(2)}, u32[]{:S(2)}) async-start(bf16[4,8,6144]{2,1,0:T(8,128)(2,1)} %bitcast.99), calls=%async_computation.3 | async-start | bytes 786432 | tf_op jit(solution)/shard_map/all_to_all | solution.py:133
  343.1 0.5 slice_bitcast_fusion.3
  343.7 6.9 %all-to-all-done.1 = bf16[4,8,6144]{2,1,0:T(8,128)(2,1)S(1)} async-done(((bf16[4,8,6144]{2,1,0:T(8,128)(2,1)}), bf16[4,8,6144]{2,1,0:T(8,128)(2,1)S(1)}, u32[]{:S(2)}, u32[]{:S(2)}) %all-to-all-start.1) | async-done | bytes 393248 | tf_op jit(solution)/shard_map/all_to_all | solution.py:133
  350.5 0.7 copy-done.2
  351.3 1.5 fusion.4
  352.8 2.8 fusion.5
  (20 shorter events, 0.1 us)
Async XLA Ops:
  6.5 210.7 %copy-start = (bf16[1,288,6144]{2,1,0:T(8,128)(2,1)S(1)}, bf16[1,288,6144]{2,1,0:T(8,128)(2,1)}, u32[]{:S(2)}) copy-start(bf16[1,288,6144]{2,1,0:T(8,128)(2,1)} %param.27) | copy-start | bytes 10616836
  6.5 62.0 %all-gather.6.cloned.1.call-start = ((), (), s32[]{:S(2)}) async-start(), calls=%async_computation.7 | async-start | bytes 8650752 | tf_op jit(solution)/shard_map/all_gather | solution.py:11
  7.9 7.3 %copy-start.6 = (f32[8]{0:T(128)}, f32[8]{0:T(128)S(1)}, u32[]{:S(2)}) copy-start(f32[8]{0:T(128)S(1)} %get-tuple-element.6) | copy-start | bytes 100
  12.9 116.2 %reduce-scatter.3.cloned.1.call-start = ((), (), s32[]{:S(2)}) async-start(), calls=%async_computation.4 | async-start | bytes 3932160 | tf_op jit(solution)/shard_map/reduce_scatter | solution.py:112
  68.5 5.2 %copy-start.3 = (bf16[256,1024]{1,0:T(8,128)(2,1)S(1)}, bf16[256,1024]{1,0:T(8,128)(2,1)}, u32[]{:S(2)}) copy-start(bf16[256,1024]{1,0:T(8,128)(2,1)} %param.14) | copy-start | bytes 1572868
  68.5 5.2 %copy-start.4 = (f32[256,8]{0,1:T(8,128)S(1)}, f32[256,8]{0,1:T(8,128)}, u32[]{:S(2)}) copy-start(f32[256,8]{0,1:T(8,128)} %get-tuple-element.11) | copy-start | bytes 24580
  73.7 2.4 copy-start.7
  76.1 3.7 %copy-start.5 = (f32[1024]{0:T(1024)S(1)}, f32[1024]{0:T(1024)}, u32[]{:S(2)}) copy-start(f32[1024]{0:T(1024)} %param.19) | copy-start | bytes 12292
  91.1 0.7 copy-start.8
  91.1 115.6 %all-gather.4.cloned.1.call-start = ((), (), s32[]{:S(2)}) async-start(), calls=%async_computation.5 | async-start | bytes 12976128 | tf_op jit(solution)/shard_map/all_gather | solution.py:125
  144.2 194.7 %reduce-scatter.5.cloned.1.call-start = ((), (), s32[]{:S(2)}) async-start(), calls=%async_computation.6 | async-start | bytes 12976128 | tf_op jit(solution)/shard_map/reduce_scatter | solution.py:126
  234.8 0.7 copy-start.9
  338.9 11.7 %all-to-all-start.1 = ((bf16[4,8,6144]{2,1,0:T(8,128)(2,1)}), bf16[4,8,6144]{2,1,0:T(8,128)(2,1)S(1)}, u32[]{:S(2)}, u32[]{:S(2)}) async-start(bf16[4,8,6144]{2,1,0:T(8,128)(2,1)} %bitcast.99), calls=%async_computation.3 | async-start | bytes 786432 | tf_op jit(solution)/shard_map/all_to_all | solution.py:133
  350.5 0.7 copy-start.2
  351.3 4.3 %copy-start.1 = (bf16[1,288,6144]{2,1,0:T(8,128)(2,1)S(1)}, bf16[1,288,6144]{2,1,0:T(8,128)(2,1)}, u32[]{:S(2)}) copy-start(bf16[1,288,6144]{2,1,0:T(8,128)(2,1)} %param.27) | copy-start | bytes 10616836
Sparse Core Ops, SparseCore 0:
  13.0 55.4 all-gather.5
  91.2 37.8 reduce-scatter.2
  144.3 62.3 all-gather.3
  235.0 103.8 reduce-scatter.4
where the time goes:
time: 363 us; the launch traced here: 362 us
  waiting for transfers between devices  258 us (71%)
  matrix products  52.1 us (14%)
  other arithmetic  15.3 us (4%)
  between operations  13.2 us (4%)
  blocking collectives  11.5 us (3%)
  local copies, waits for them, and re-layouts  7.34 us (2%)
  starting transfers between devices  4.58 us (1%)
    reduce_scatter x1, waiting for transfers between devices, body(): lax.psum_scatter(expert_part(gathered, w_gate[0], w_up[0], w_down[0]).ast...  103 us
    all_gather x1, waiting for transfers between devices, body(): gathered = lax.all_gather(mine, 'ctx', axis=0, tiled=True)  62.3 us
    all_gather x1, waiting for transfers between devices, earlier_states(): lax.all_gather(update.astype(jnp.bfloat16), 'ctx').astype(jnp.float32)  48.4 us
    reduce_scatter x1, waiting for transfers between devices, body(): lax.psum_scatter(projected.astype(jnp.bfloat16), 'exp', scatter_dimension...  37 us
    dot_general x1, matrix products, expert_part(): return jnp.dot(activated, down_rows, preferred_element_type=jnp.float32)  17.6 us
    all_to_all x1, blocking collectives, body(): mine = lax.all_to_all(outgoing, 'exp', 0, 0, tiled=True)  11.5 us
    dot_general x1, matrix products, expert_part(): lax.dot_general(slot_rows, gate_cols, contract_dims, preferred_element_ty...  10.5 us
    dot_general x1, matrix products, body(): projected = jnp.dot(settled, out_proj, preferred_element_type=jnp.float32)  9.51 us
  transfers between devices with their start and end apart: 5, of which 5 were waited for; matrix products, arithmetic and copies ran while one was open for 2% of the time, Pallas kernels for 0%

commit v1 on v0

--- a/solution.py
+++ b/solution.py
@@ -122,7 +122,9 @@
     ).astype(jnp.bfloat16)
     mine = lax.all_to_all(outgoing, "exp", 0, 0, tiled=True)
     mine = mine.reshape(group_count * capacity, -1)
-    gathered = lax.all_gather(mine, "ctx", axis=0, tiled=True)
+    gathered = jnp.concatenate(
+        lax.all_to_all(jnp.stack([mine] * lax.axis_size("ctx")), "ctx", 0, 0), axis=0
+    )
     produced = lax.psum_scatter(
         expert_part(gathered, w_gate[0], w_up[0], w_down[0]).astype(jnp.bfloat16),
         "ctx",

time: 363 us -> 451 us (1.24)
  blocking collectives: 11.5 us -> 159 us
  waiting for transfers between devices: 258 us -> 195 us
  local copies, waits for them, and re-layouts: 7.34 us -> 17.2 us
  matrix products: 52.1 us -> 46.1 us
    all_to_all x0 -> x1, blocking collectives: none -> 148 us  [body(): lax.all_to_all(jnp.stack([mine] * lax.axis_size('ctx')), 'ctx', 0, 0)]
    all_gather x1 -> x0, waiting for transfers between devices: 62.3 us -> none  [body(): gathered = lax.all_gather(mine, 'ctx', axis=0, tiled=True)]
    another operation x0 -> x1, local copies, waits for them, and re-layouts: none -> 6.1 us  [body(): jnp.stack([mine] * lax.axis_size('ctx'))]
    dot_general x1, matrix products: 10.5 us -> 4.99 us  [expert_part(): lax.dot_general(slot_rows, gate_cols, contract_dims, preferred_element_ty...]
  transfers between devices with their start and end apart: 5 -> 4, of which waited for: 5 -> 4; matrix products, arithmetic and copies ran while one was open for 2% -> 2% of each run, Pallas kernels for 0% -> 0%
where the time goes in v1:
time: 451 us; the launch traced here: 450 us
  waiting for transfers between devices  195 us (43%)
  blocking collectives  159 us (35%)
  matrix products  46.1 us (10%)
  local copies, waits for them, and re-layouts  17.2 us (4%)
  other arithmetic  15.2 us (3%)
  between operations  13.2 us (3%)
    all_to_all x1, blocking collectives, body(): lax.all_to_all(jnp.stack([mine] * lax.axis_size('ctx')), 'ctx', 0, 0)  148 us
    reduce_scatter x1, waiting for transfers between devices, body(): lax.psum_scatter(expert_part(gathered, w_gate[0], w_up[0], w_down[0]).ast...  102 us
    all_gather x1, waiting for transfers between devices, earlier_states(): lax.all_gather(update.astype(jnp.bfloat16), 'ctx').astype(jnp.float32)  48.5 us
    reduce_scatter x1, waiting for transfers between devices, body(): lax.psum_scatter(projected.astype(jnp.bfloat16), 'exp', scatter_dimension...  37.1 us
    dot_general x1, matrix products, expert_part(): return jnp.dot(activated, down_rows, preferred_element_type=jnp.float32)  17.6 us
    all_to_all x1, blocking collectives, body(): mine = lax.all_to_all(outgoing, 'exp', 0, 0, tiled=True)  10.8 us
    dot_general x1, matrix products, body(): projected = jnp.dot(settled, out_proj, preferred_element_type=jnp.float32)  9.5 us
  transfers between devices with their start and end apart: 4, of which 4 were waited for; matrix products, arithmetic and copies ran while one was open for 2% of the time, Pallas kernels for 0%

profile of v1, /device:TPU:0, one launch (start us, length us, event | category | flops | bytes accessed | tf_op | source)
XLA Modules:
  0.0 449.9 jit_solution(17354733472904034027)
XLA Ops:
  6.5 0.0 copy-start
  6.5 1.3 broadcast_multiply_fusion
  7.9 2.0 copy.27
  9.9 0.7 multiply_exponential_fusion
  10.6 2.2 convolution_convert_fusion.3
  12.8 0.0 all-gather.3.cloned.1.call-update
  12.8 0.0 reduce-scatter.3.cloned.1.call-start
  12.9 2.3 add_divide_fusion
  15.2 2.6 copy.25
  17.8 0.7 fusion.46
  18.5 0.8 fusion.45
  19.3 0.7 exponential_select_fusion
  20.0 48.5 %all-gather.3.cloned.1.call-done = bf16[256,128,128]{2,1,0:T(8,128)(2,1)} async-done(((bf16[8,128,128]{2,1,0:T(8,128)(2,1)}), bf16[256,128,128]{2,1,0:T(8,128)(2,1)}) %all-gather.3.cloned.1.call-update) | async-done | bytes 8388624 | tf_op jit(solution)/shard_map/all_gather | solution.py:11
  68.5 5.2 %fusion = f32[8,128,128]{2,1,0:T(8,128)S(1)} fusion(bf16[32,8,128,128]{3,2,1,0:T(8,128)(2,1)} %bitcast.96, f32[32,8]{1,0:T(8,128)S(1)} %exponential_select_fusion), kind=kLoop, calls=%fused_computation.1 | loop fusion | flops 12451840 | bytes 8913920 | tf_op jit(solution)/shard_map/reduce_sum | solution.py:18
  73.7 0.0 copy-start.8
  73.7 0.0 copy-done.4
  73.7 0.0 copy-done.5
  73.7 2.4 convolution_bitcast_fusion.2
  76.1 3.7 multiply_reduce_fusion.1
  79.8 1.8 multiply_convert_fusion.2
  81.5 9.5 %convolution_convert_fusion.1 = bf16[256,6144]{1,0:T(8,128)(2,1)} fusion(bf16[256,1024]{0,1:T(8,128)(2,1)S(1)} %bitcast.98, bf16[1024,6144]{1,0:T(8,128)(2,1)} %param.20), kind=kOutput, calls=%fused_computation.3 | convolution fusion | flops 3222798336 | bytes 16252928 | tf_op jit(solution)/shard_map/dot_general | solution.py:111
  91.1 0.0 reduce-scatter.3.cloned.1.call-update
  91.1 0.0 reduce-scatter.5.cloned.1.call-start
  91.1 0.6 copy-done.9
  91.7 0.1 constant_dynamic-slice_fusion
  91.8 0.1 iota_compare_fusion.3
  91.9 0.1 convolution_add_fusion
  92.0 37.1 %reduce-scatter.3.cloned.1.call-done = bf16[64,6144]{1,0:T(8,128)(2,1)} async-done(((bf16[256,6144]{1,0:T(8,128)(2,1)}), bf16[64,6144]{1,0:T(8,128)(2,1)}) %reduce-scatter.3.cloned.1.call-update) | async-done | bytes 786448 | tf_op jit(solution)/shard_map/reduce_scatter | solution.py:112
  129.1 1.7 multiply_reduce_fusion
  130.8 1.8 convolution_convert_fusion.2
  132.6 10.8 %all_to_all.15 = bf16[4,8,6144]{2,1,0:T(8,128)(2,1)S(1)} all-to-all(bf16[4,8,6144]{2,1,0:T(8,128)(2,1)S(1)} %convolution_convert_fusion.2), channel_id=1, replica_groups=mesh['ctx'=32,'exp'=4] {'exp'}, dimensions={0} | all-to-all | bytes 786432 | tf_op jit(solution)/shard_map/all_to_all | solution.py:123
  143.4 6.1 %stack.3 = bf16[32,32,6144]{2,1,0:T(8,128)(2,1)} broadcast(bf16[32,6144]{1,0:T(8,128)(2,1)S(1)} %bitcast.99), dimensions={1,2} | broadcast | bytes 12976128 | tf_op jit(solution)/shard_map/stack | solution.py:126
  149.5 148.4 %all_to_all.16 = bf16[32,32,6144]{2,1,0:T(8,128)(2,1)S(1)} all-to-all(bf16[32,32,6144]{2,1,0:T(8,128)(2,1)} %stack.3), channel_id=1, replica_groups=mesh['ctx'=32,'exp'=4] {'ctx'}, dimensions={0} | all-to-all | bytes 25165824 | tf_op jit(solution)/shard_map/all_to_all | solution.py:126
  298.0 4.5 copy-done.1
  302.4 0.0 copy-done.11
  302.4 5.0 %fusion.9 = f32[1024,288]{0,1:T(8,128)} fusion(bf16[1024,6144]{1,0:T(8,128)(2,1)S(1)} %bitcast.94, bf16[1,288,6144]{2,1,0:T(8,128)(2,1)S(1)} %copy-done.11), kind=kOutput, calls=%fused_computation.15 | convolution fusion | flops 3623878656 | bytes 17301504 | tf_op jit(solution)/shard_map/dot_general | solution.py:77
  307.4 17.6 %convolution_convert_fusion = bf16[1024,6144]{1,0:T(8,128)(2,1)} fusion(bf16[1,288,6144]{2,1,0:T(8,128)(2,1)S(1)} %copy-done, bf16[1024,6144]{1,0:T(8,128)(2,1)} %bitcast.95, bf16[1,288,6144]{2,1,0:T(8,128)(2,1)} %param.26, f32[1024,288]{0,1:T(8,128)} %fusion.9), kind=kOutput, calls=%fused_computation.2 | convolution fusion | flops 7255818240 | bytes 33423360 | tf_op jit(solution)/shard_map/dot_general | solution.py:84
  325.1 0.0 reduce-scatter.5.cloned.1.call-update
  325.1 0.7 copy-done.10
  325.8 0.1 constant_dynamic-slice_fusion.1
  325.8 102.0 %reduce-scatter.5.cloned.1.call-done = bf16[32,6144]{1,0:T(8,128)(2,1)} async-done(((bf16[1024,6144]{1,0:T(8,128)(2,1)}), bf16[32,6144]{1,0:T(8,128)(2,1)}) %reduce-scatter.5.cloned.1.call-update) | async-done | bytes 393232 | tf_op jit(solution)/shard_map/reduce_scatter | solution.py:128
  427.8 4.3 all-to-all-start.2
  432.1 0.5 slice_bitcast_fusion.3
  432.6 7.0 %all-to-all-done.2 = bf16[4,8,6144]{2,1,0:T(8,128)(2,1)} async-done(((bf16[4,8,6144]{2,1,0:T(8,128)(2,1)}), bf16[4,8,6144]{2,1,0:T(8,128)(2,1)}, u32[]{:S(2)}, u32[]{:S(2)}) %all-to-all-start.2) | async-done | bytes 393248 | tf_op jit(solution)/shard_map/all_to_all | solution.py:135
  439.6 1.5 fusion.4
  441.1 0.0 copy-done.2
  441.1 0.0 copy-done.3
  441.1 2.3 fusion.5
  (23 shorter events, 0.1 us)
Async XLA Ops:
  6.5 300.9 %copy-start = (bf16[1,288,6144]{2,1,0:T(8,128)(2,1)S(1)}, bf16[1,288,6144]{2,1,0:T(8,128)(2,1)}, u32[]{:S(2)}) copy-start(bf16[1,288,6144]{2,1,0:T(8,128)(2,1)} %param.27) | copy-start | bytes 10616836
  6.5 62.0 %all-gather.3.cloned.1.call-start = ((), (), s32[]{:S(2)}) async-start(), calls=%async_computation.7 | async-start | bytes 8650752 | tf_op jit(solution)/shard_map/all_gather | solution.py:11
  7.9 7.3 %copy-start.7 = (f32[8]{0:T(128)}, f32[8]{0:T(128)S(1)}, u32[]{:S(2)}) copy-start(f32[8]{0:T(128)S(1)} %get-tuple-element.6) | copy-start | bytes 100
  12.8 116.2 %reduce-scatter.3.cloned.1.call-start = ((), (), s32[]{:S(2)}) async-start(), calls=%async_computation.5 | async-start | bytes 3932160 | tf_op jit(solution)/shard_map/reduce_scatter | solution.py:112
  68.5 5.2 %copy-start.4 = (bf16[256,1024]{1,0:T(8,128)(2,1)S(1)}, bf16[256,1024]{1,0:T(8,128)(2,1)}, u32[]{:S(2)}) copy-start(bf16[256,1024]{1,0:T(8,128)(2,1)} %param.14) | copy-start | bytes 1572868
  68.5 5.2 %copy-start.5 = (f32[256,8]{0,1:T(8,128)S(1)}, f32[256,8]{0,1:T(8,128)}, u32[]{:S(2)}) copy-start(f32[256,8]{0,1:T(8,128)} %get-tuple-element.11) | copy-start | bytes 24580
  73.7 2.4 copy-start.8
  76.1 3.7 copy-start.6
  91.1 0.7 copy-start.9
  91.1 336.8 %reduce-scatter.5.cloned.1.call-start = ((), (), s32[]{:S(2)}) async-start(), calls=%async_computation.6 | async-start | bytes 12976128 | tf_op jit(solution)/shard_map/reduce_scatter | solution.py:128
  149.5 152.9 %copy-start.11 = (bf16[1,288,6144]{2,1,0:T(8,128)(2,1)S(1)}, bf16[1,288,6144]{2,1,0:T(8,128)(2,1)}, u32[]{:S(2)}) copy-start(bf16[1,288,6144]{2,1,0:T(8,128)(2,1)} %param.25) | copy-start | bytes 10616836
  298.0 4.5 copy-start.1
  325.1 0.7 copy-start.10
  427.8 11.8 %all-to-all-start.2 = ((bf16[4,8,6144]{2,1,0:T(8,128)(2,1)}), bf16[4,8,6144]{2,1,0:T(8,128)(2,1)}, u32[]{:S(2)}, u32[]{:S(2)}) async-start(bf16[4,8,6144]{2,1,0:T(8,128)(2,1)} %bitcast.102), calls=%async_computation.4 | async-start | bytes 786432 | tf_op jit(solution)/shard_map/all_to_all | solution.py:135
  439.6 1.5 copy-start.2
  439.6 1.5 copy-start.3
Sparse Core Ops, SparseCore 0:
  13.0 55.4 all-gather.2
  91.2 37.8 reduce-scatter.2
  325.2 102.5 reduce-scatter.4
